TPU v7x, 32 devices: a whole 2x2x4 slice. The times are simulated.
32 devices in a mesh: ctx: 16 (over z, y, core), tp: 2 (over x).
Axes of the slice: x: 2, y: 2, z: 4, core: 2. Of those that a mesh axis runs over, the one named last changes fastest.
Arguments:
- tokens: bfloat16 [4096, 1024], P('ctx'), may hold values from -6 to 6
- seq_ids: int32 [4096], P('ctx'), may hold values from 0 to 3, never falling along the last dimension, each value on 1 to 2048 neighbouring positions
- attention_norm_gain: float32 [1024], replicated, may hold values from 0.5 to 1.5
- qkv_weight: bfloat16 [1024, 3, 1024], P(None, None, 'tp'), may hold values from -1 to 1, as said below
- out_weight: bfloat16 [1024, 1024], P('tp'), may hold values from -1.5 to 1.5
- feedforward_norm_gain: float32 [1024], replicated, may hold values from 0.5 to 1.5
- mlp_in_weight: bfloat16 [1024, 2, 2624], P(None, None, 'tp'), may hold values from -0.1875 to 0.1875
- mlp_out_weight: bfloat16 [2624, 1024], P('tp'), may hold values from -0.125 to 0.125
- grad_out: bfloat16 [4096, 1024], P('ctx'), may hold values from -6 to 6
Outputs:
- output: bfloat16 [4096, 1024], P('ctx')
- grad_tokens: float32 [4096, 1024], P('ctx')
- grad_norm1_gain: float32 [1024], replicated
- grad_qkv_weight: float32 [1024, 3, 1024], P(None, None, 'tp')
- grad_out_weight: float32 [1024, 1024], P('tp')
- grad_norm2_gain: float32 [1024], replicated
- grad_mlp_in_weight: float32 [1024, 2, 2624], P(None, None, 'tp')
- grad_mlp_out_weight: float32 [2624, 1024], P('tp')
Inputs may be any that keep to these rules, and one draw needn't show every extreme that they name: `seq_ids`: never falling along the tokens; every one of the 4 sequences has at least one token and one has exactly 2048. `qkv_weight`: A projection matrix with entries of order 1024^(-1/2).
All inputs are finite; a program needn't handle non-finite values.
Results may differ from a plain program's by a relative error of at most 0.025.
Values may be sent and summed in bfloat16 or wider, within the bound.
No kernel may reach another device: no remote copies, remote signals or barrier semaphores. Data moves between devices by JAX's collectives and lax.ppermute only.
A program may use at most 256 MiB of HBM per device.

v0:
```python
import math
import jax
import jax.numpy as jnp
from jax import lax
from jax.sharding import PartitionSpec as P

HD = 64
EPS = 1e-05
BASE = 160000.0
MASKED = -1e30
ROOT_HALF = 0.7071067811865476
INV_ROOT_TWO_PI = 0.3989422804014327


def layer_normalize(values_in, norm_gain_vector):
    token_average = jnp.mean(values_in, axis=-1, keepdims=True)
    centered_input = values_in - token_average
    inverse_deviation = lax.rsqrt(
        jnp.mean(centered_input * centered_input, axis=-1, keepdims=True) + EPS
    )
    standardized_input = centered_input * inverse_deviation
    return (standardized_input, inverse_deviation, standardized_input * norm_gain_vector)


def layer_normalize_backward(
    output_gradient, standardized_input, inverse_deviation, norm_gain_vector
):
    normalized_gradient = output_gradient * norm_gain_vector
    correction_term = jnp.mean(
        normalized_gradient, axis=-1, keepdims=True
    ) + standardized_input * jnp.mean(
        normalized_gradient * standardized_input, axis=-1, keepdims=True
    )
    return (
        inverse_deviation * (normalized_gradient - correction_term),
        jnp.sum(output_gradient * standardized_input, axis=0),
    )


def gelu_value(v):
    return v * 0.5 * (1.0 + lax.erf(v * ROOT_HALF))


def gelu_slope(v):
    return 0.5 * (1.0 + lax.erf(v * ROOT_HALF)) + v * jnp.exp(-0.5 * v * v) * INV_ROOT_TWO_PI


def rope_tables(positions, head_size):
    half = head_size // 2
    inverse = BASE ** (-(jnp.arange(half, dtype=jnp.float32) * (2.0 / head_size)))
    angle = positions.astype(jnp.float32)[:, None] * inverse[None, :]
    angle = jnp.concatenate([angle, angle], axis=-1)
    return (jnp.cos(angle), jnp.sin(angle))


def rotate(field, cosine, sine):
    half = field.shape[-1] // 2
    turned = jnp.concatenate([-field[..., half:], field[..., :half]], axis=-1)
    return field * cosine[:, None, :] + turned * sine[:, None, :]


def unrotate(grad, cosine, sine):
    half = grad.shape[-1] // 2
    lifted = grad * sine[:, None, :]
    back = jnp.concatenate([lifted[..., half:], -lifted[..., :half]], axis=-1)
    return grad * cosine[:, None, :] + back


def block_grads(q_rows, do_rows, lse_rows, delta_rows, seq_rows, k_rows, v_rows, seq_cols, scale):
    f32 = jnp.float32
    scores = jnp.einsum("qhd,khd->hqk", q_rows, k_rows, preferred_element_type=f32) * scale
    same = (seq_rows[:, None] == seq_cols[None, :])[None]
    probs = jnp.where(same, jnp.exp(scores - lse_rows.T[:, :, None]), 0.0)
    grad_v = jnp.einsum(
        "hqk,qhd->khd", probs.astype(jnp.bfloat16), do_rows, preferred_element_type=f32
    )
    grad_p = jnp.einsum("qhd,khd->hqk", do_rows, v_rows, preferred_element_type=f32)
    grad_s = (probs * (grad_p - delta_rows.T[:, :, None])).astype(jnp.bfloat16)
    grad_q = jnp.einsum("hqk,khd->qhd", grad_s, k_rows, preferred_element_type=f32) * scale
    grad_k = jnp.einsum("hqk,qhd->khd", grad_s, q_rows, preferred_element_type=f32) * scale
    return (grad_q, grad_k, grad_v)


def per_device(
    tokens,
    seq_ids,
    attention_norm_gain,
    qkv_weight,
    out_weight,
    feedforward_norm_gain,
    mlp_in_weight,
    mlp_out_weight,
    grad_out,
):
    f32 = jnp.float32
    bf16 = jnp.bfloat16
    tok_rows, width = tokens.shape
    local_cols = qkv_weight.shape[2]
    heads_here = local_cols // HD
    hidden_here = mlp_in_weight.shape[2]
    scale = 1.0 / math.sqrt(HD)
    input_tokens = tokens.astype(f32)
    attention_standardized, attention_inverse_deviation, attention_normed_input = layer_normalize(
        input_tokens, attention_norm_gain
    )
    first = attention_normed_input.astype(bf16)
    qkv_flat = qkv_weight.reshape(width, 3 * local_cols)
    proj = jnp.dot(first, qkv_flat, preferred_element_type=f32).reshape(tok_rows, 3, heads_here, HD)
    positions = lax.axis_index("ctx") * tok_rows + jnp.arange(tok_rows, dtype=jnp.int32)
    cosine, sine = rope_tables(positions, HD)
    query = rotate(proj[:, 0], cosine, sine).astype(bf16)
    keys = rotate(proj[:, 1], cosine, sine).astype(bf16)
    values = proj[:, 2].astype(bf16)
    keys_flat = keys.reshape(tok_rows, local_cols)
    values_flat = values.reshape(tok_rows, local_cols)
    run_max = jnp.full((heads_here, tok_rows), MASKED, f32)
    key_piece = lax.all_gather(keys_flat, "ctx", axis=0, tiled=True)
    value_piece = lax.all_gather(values_flat, "ctx", axis=0, tiled=True)
    seq_piece = lax.all_gather(seq_ids, "ctx", axis=0, tiled=True)
    count = key_piece.shape[0]
    key_heads = key_piece.reshape(count, heads_here, HD)
    value_heads = value_piece.reshape(count, heads_here, HD)
    scores = jnp.einsum("qhd,khd->hqk", query, key_heads, preferred_element_type=f32) * scale
    same = (seq_ids[:, None] == seq_piece[None, :])[None]
    top = jnp.max(jnp.where(same, scores, MASKED), axis=-1)
    new_max = jnp.maximum(run_max, top)
    weights = jnp.where(same, jnp.exp(scores - new_max[..., None]), 0.0)
    run_sum = jnp.sum(weights, axis=-1)
    added = jnp.einsum(
        "hqk,khd->hqd", weights.astype(bf16), value_heads, preferred_element_type=f32
    )
    run_acc = added
    run_max, run_sum, run_acc = (new_max, run_sum, run_acc)
    attended = (run_acc / run_sum[..., None]).transpose(1, 0, 2).astype(bf16)
    lse = (run_max + jnp.log(run_sum)).T
    attended_flat = attended.reshape(tok_rows, local_cols)
    attn_part = jnp.dot(attended_flat, out_weight, preferred_element_type=f32)
    residual_middle = input_tokens + lax.psum(attn_part.astype(jnp.bfloat16), "tp").astype(
        jnp.float32
    )
    feedforward_standardized, feedforward_inverse_deviation, feedforward_normed_input = (
        layer_normalize(residual_middle, feedforward_norm_gain)
    )
    second = feedforward_normed_input.astype(bf16)
    in_flat = mlp_in_weight.reshape(width, 2 * hidden_here)
    mixed = jnp.dot(second, in_flat, preferred_element_type=f32).reshape(tok_rows, 2, hidden_here)
    act_in = mixed[:, 0]
    gate = mixed[:, 1]
    hidden = (gelu_value(act_in) * gate).astype(bf16)
    ffn_part = jnp.dot(hidden, mlp_out_weight, preferred_element_type=f32)
    output = (
        residual_middle + lax.psum(ffn_part.astype(jnp.bfloat16), "tp").astype(jnp.float32)
    ).astype(bf16)
    upstream = grad_out.astype(f32)
    grad_w_out = jnp.dot(hidden.T, grad_out, preferred_element_type=f32)
    grad_hidden = jnp.dot(grad_out, mlp_out_weight.T, preferred_element_type=f32)
    grad_mixed = jnp.stack(
        [grad_hidden * gate * gelu_slope(act_in), grad_hidden * gelu_value(act_in)], axis=1
    ).astype(bf16)
    grad_mixed_flat = grad_mixed.reshape(tok_rows, 2 * hidden_here)
    grad_w_in = jnp.dot(second.T, grad_mixed_flat, preferred_element_type=f32).reshape(
        width, 2, hidden_here
    )
    second_part = jnp.dot(grad_mixed_flat, in_flat.T, preferred_element_type=f32)
    feedforward_norm_gradient = lax.psum(second_part.astype(jnp.bfloat16), "tp").astype(jnp.float32)
    feedforward_normed_gradient, feedforward_gain_gradient = layer_normalize_backward(
        feedforward_norm_gradient,
        feedforward_standardized,
        feedforward_inverse_deviation,
        feedforward_norm_gain,
    )
    grad_mid = upstream + feedforward_normed_gradient
    grad_mid_b = grad_mid.astype(bf16)
    grad_w_attn = jnp.dot(attended_flat.T, grad_mid_b, preferred_element_type=f32)
    grad_att = (
        jnp.dot(grad_mid_b, out_weight.T, preferred_element_type=f32)
        .astype(bf16)
        .reshape(tok_rows, heads_here, HD)
    )
    delta = jnp.sum(grad_att.astype(f32) * attended.astype(f32), axis=-1)
    key_piece = lax.all_gather(keys_flat, "ctx", axis=0, tiled=True)
    value_piece = lax.all_gather(values_flat, "ctx", axis=0, tiled=True)
    seq_piece = lax.all_gather(seq_ids, "ctx", axis=0, tiled=True)
    count = key_piece.shape[0]
    key_heads = key_piece.reshape(count, heads_here, HD)
    value_heads = value_piece.reshape(count, heads_here, HD)
    gq, gk, gv = block_grads(
        query, grad_att, lse, delta, seq_ids, key_heads, value_heads, seq_piece, scale
    )
    pair = jnp.stack([gk.reshape(count, local_cols), gv.reshape(count, local_cols)], axis=1)
    own_pairs = lax.psum_scatter(
        pair.astype(jnp.bfloat16), "ctx", scatter_dimension=0, tiled=True
    ).astype(jnp.float32)
    grad_key = own_pairs[:, 0].reshape(tok_rows, heads_here, HD)
    grad_value = own_pairs[:, 1].reshape(tok_rows, heads_here, HD)
    grad_proj = jnp.stack(
        [unrotate(gq, cosine, sine), unrotate(grad_key, cosine, sine), grad_value], axis=1
    )
    grad_proj = grad_proj.astype(bf16).reshape(tok_rows, 3 * local_cols)
    grad_w_qkv = jnp.dot(first.T, grad_proj, preferred_element_type=f32).reshape(
        width, 3, local_cols
    )
    first_part = jnp.dot(grad_proj, qkv_flat.T, preferred_element_type=f32)
    attention_norm_gradient = lax.psum(first_part.astype(jnp.bfloat16), "tp").astype(jnp.float32)
    attention_normed_gradient, attention_gain_gradient = layer_normalize_backward(
        attention_norm_gradient,
        attention_standardized,
        attention_inverse_deviation,
        attention_norm_gain,
    )
    grad_tokens = grad_mid + attention_normed_gradient
    summed = (
        lax.psum(attention_gain_gradient.astype(jnp.bfloat16), "ctx").astype(jnp.float32),
        lax.psum(grad_w_qkv.astype(jnp.bfloat16), "ctx").astype(jnp.float32),
        lax.psum(grad_w_attn.astype(jnp.bfloat16), "ctx").astype(jnp.float32),
        lax.psum(feedforward_gain_gradient.astype(jnp.bfloat16), "ctx").astype(jnp.float32),
        lax.psum(grad_w_in.astype(jnp.bfloat16), "ctx").astype(jnp.float32),
        lax.psum(grad_w_out.astype(jnp.bfloat16), "ctx").astype(jnp.float32),
    )
    return (output, grad_tokens, summed[0], summed[1], summed[2], summed[3], summed[4], summed[5])


def solution(mesh):
    return jax.shard_map(
        per_device,
        mesh=mesh,
        in_specs=(
            P("ctx", None),
            P("ctx"),
            P(),
            P(None, None, "tp"),
            P("tp", None),
            P(),
            P(None, None, "tp"),
            P("tp", None),
            P("ctx", None),
        ),
        out_specs=(
            P("ctx", None),
            P("ctx", None),
            P(),
            P(None, None, "tp"),
            P("tp", None),
            P(),
            P(None, None, "tp"),
            P("tp", None),
        ),
        check_vma=False,
    )
```

profile of v0, /device:TPU:0, one launch (start us, length us, event | category | flops | bytes accessed | tf_op | source)
XLA Modules:
  0.0 697.2 jit_solution(1876158596142752087)
XLA Ops:
  7.3 4.8 copy.22
  12.6 3.0 fusion.57
  24.1 23.5 %all-gather = s32[16,1,256]{2,1,0:T(1,128)S(1)} all-gather(s32[1,1,256]{2,1,0:T(1,128)S(1)} %bitcast.163), channel_id=1, replica_groups=mesh['ctx'=16,'tp'=2] {'ctx'}, dimensions={0}, use_global_device_ids=true | all-gather | bytes 17408 | tf_op jit(solution)/shard_map/all_gather | solution.py:119
  49.2 28.3 %all-gather.4.cloned.1.call-done = bf16[4096,512]{0,1:T(8,128)(2,1)} async-done(((bf16[256,512]{0,1:T(8,128)(2,1)}), bf16[4096,512]{0,1:T(8,128)(2,1)}) %all-gather.4.cloned.1.call-update) | async-done | bytes 4194320 | tf_op jit(solution)/shard_map/all_gather | solution.py:117
  77.5 16.5 %select_reduce_fusion = (f32[8,256]{1,0:T(8,128)S(1)}, f32[8,256,4096]{2,1,0:T(8,128)}) fusion(pred[256,4096]{1,0:T(8,128)(4,1)} %broadcast_compare_fusion, bf16[256,8,64]{0,2,1:T(8,128)(2,1)S(1)} %get-tuple-element.38, bf16[4096,8,64]{0,2,1:T(8,128)(2,1)} %bitcast.142), kind=kOutput, calls=%fused_computation.3 | convolution fusion | flops 1098905600 | bytes 39067648 | tf_op jit(solution)/shard_map/qhd,khd->hqk/dot_general | solution.py:123
  94.6 16.2 %fusion = f32[8,256]{1,0:T(8,128)} fusion(f32[8,256,4096]{2,1,0:T(8,128)} %get-tuple-element.44, f32[8,256]{1,0:T(8,128)S(1)} %broadcast_maximum_fusion, pred[256,4096]{1,0:T(8,128)(4,1)S(1)} %copy-done.4), kind=kLoop, calls=%fused_computation.4 | loop fusion | flops 33552384 | bytes 34619392 | tf_op jit(solution)/shard_map/reduce_sum | solution.py:128
  110.8 20.1 %all-gather.6.cloned.1.call-done = bf16[4096,512]{0,1:T(8,128)(2,1)} async-done(((bf16[256,512]{0,1:T(8,128)(2,1)}), bf16[4096,512]{0,1:T(8,128)(2,1)}) %all-gather.6.cloned.1.call-update) | async-done | bytes 4194320 | tf_op jit(solution)/shard_map/all_gather | solution.py:118
  130.9 16.3 %fusion.49 = bf16[256,8,64]{0,2,1:T(8,128)(2,1)} fusion(bf16[4096,8,64]{0,2,1:T(8,128)(2,1)} %bitcast.164, f32[8,256,4096]{2,1,0:T(8,128)} %get-tuple-element.44, f32[8,256]{1,0:T(8,128)} %copy-done.29, pred[256,4096]{1,0:T(8,128)(4,1)} %broadcast_compare_fusion, f32[256,8]{0,1:T(8,128)} %bitcast.161), kind=kOutput, calls=%fused_computation.78 | convolution fusion | flops 1107558400 | bytes 39075840 | tf_op jit(solution)/shard_map/hqk,khd->hqd/dot_general | solution.py:129
  147.2 2.6 convolution_convert_fusion.4
  150.4 26.4 %all-reduce.8.cloned.1.call-done = bf16[256,1024]{1,0:T(8,128)(2,1)} async-done(((bf16[256,1024]{1,0:T(8,128)(2,1)}), bf16[256,1024]{1,0:T(8,128)(2,1)}) %all-reduce.8.cloned.1.call-update) | async-done | bytes 524304 | tf_op jit(solution)/shard_map/psum | solution.py:138
  179.5 4.5 fusion.12
  186.6 5.0 fusion.27
  193.0 27.5 %all-reduce.10.cloned.1.call-done = bf16[256,1024]{1,0:T(8,128)(2,1)} async-done(((bf16[256,1024]{1,0:T(8,128)(2,1)}), bf16[256,1024]{1,0:T(8,128)(2,1)}) %all-reduce.10.cloned.1.call-update) | async-done | bytes 524304 | tf_op jit(solution)/shard_map/psum | solution.py:165
  220.5 2.5 fusion.41
  222.9 1.8 fusion.40
  229.9 19.3 %fusion.9 = bf16[8,64,4096]{2,1,0:T(8,128)(2,1)} fusion(bf16[256,8,64]{0,2,1:T(8,128)(2,1)} %bitcast.158, f32[8,256,4096]{2,1,0:T(8,128)} %get-tuple-element.44, f32[8,256]{1,0:T(8,128)} %log_add_fusion, pred[256,4096]{1,0:T(8,128)(4,1)} %broadcast_compare_fusion), kind=kOutput, calls=%fused_computation.13 | convolution fusion | flops 1109393408 | bytes 39067648 | tf_op jit(solution)/shard_map/hqk,qhd->khd/dot_general | solution.py:74
  249.2 23.4 %multiply_convert_fusion = bf16[8,256,4096]{2,1,0:T(8,128)(2,1)} fusion(f32[8,256,4096]{2,1,0:T(8,128)} %get-tuple-element.44, f32[8,256]{1,0:T(8,128)S(1)} %bitcast.162, f32[8,256]{1,0:T(8,128)} %log_add_fusion, pred[256,4096]{1,0:T(8,128)(4,1)} %broadcast_compare_fusion, bf16[256,8,64]{0,2,1:T(8,128)(2,1)} %bitcast.159, bf16[4096,8,64]{0,2,1:T(8,128)(2,1)} %bitcast.165), kind=kOutput, calls=%fused_computation | convolution fusion | flops 1124073472 | bytes 55853056 | tf_op jit(solution)/shard_map/qhd,khd->hqk/dot_general | solution.py:77
  272.6 10.8 %multiply_convert_fusion.1 = bf16[8,64,4096]{2,1,0:T(8,128)(2,1)} fusion(bf16[256,8,64]{0,2,1:T(8,128)(2,1)S(1)} %get-tuple-element.38, bf16[8,256,4096]{2,1,0:T(8,128)(2,1)} %multiply_convert_fusion), kind=kOutput, calls=%fused_computation.12 | convolution fusion | flops 1077936128 | bytes 21233664 | tf_op jit(solution)/shard_map/hqk,qhd->khd/dot_general | solution.py:80
  283.4 7.6 %pad_maximum_fusion = bf16[4096,2,512]{0,2,1:T(8,128)(2,1)} fusion(bf16[4096,1,512]{0,2,1:T(8,128)(2,1)} %bitcast.149, bf16[4096,1,512]{0,2,1:T(8,128)(2,1)} %bitcast.144), kind=kLoop, calls=%fused_computation.11 | loop fusion | flops 4194304 | bytes 16777216 | tf_op jit(solution)/shard_map/stack | solution.py:190
  291.3 2.0 multiply_convert_fusion.2
  296.0 15.0 %broadcast_multiply_fusion = (f32[256,8,64]{0,2,1:T(8,128)}, f32[256,8,64]{0,2,1:T(8,128)}) fusion(f32[256,64]{0,1:T(8,128)S(1)} %copy-done.22, bf16[4096,8,64]{0,2,1:T(8,128)(2,1)} %bitcast.143, bf16[8,256,4096]{2,1,0:T(8,128)(2,1)} %multiply_convert_fusion), kind=kOutput, calls=%fused_computation.103 | convolution fusion | flops 1073872896 | bytes 22085632 | tf_op jit(solution)/shard_map/hqk,khd->qhd/dot_general | solution.py:79
  313.3 81.5 %reduce-scatter.2.cloned.1.call-done = bf16[256,2,512]{0,2,1:T(8,128)(2,1)} async-done(((bf16[4096,2,512]{0,2,1:T(8,128)(2,1)}), bf16[256,2,512]{0,2,1:T(8,128)(2,1)}) %reduce-scatter.2.cloned.1.call-update) | async-done | bytes 524304 | tf_op jit(solution)/shard_map/reduce_scatter | solution.py:191
  399.9 3.8 convolution_convert_fusion.1
  403.7 4.2 convolution_convert_fusion
  409.3 2.9 convolution_convert_fusion.2
  412.2 27.5 %all-reduce.14.cloned.1.call-done = (bf16[256,1024]{1,0:T(8,128)(2,1)}, bf16[256,1024]{1,0:T(8,128)(2,1)}) async-done(((bf16[256,1024]{1,0:T(8,128)(2,1)}, bf16[256,1024]{1,0:T(8,128)(2,1)}), (bf16[256,1024]{1,0:T(8,128)(2,1)}, bf16[256,1024]{1,0:T(8,128)(2,1)})) %all-reduce.14.cloned.1.call-update) | async-done | bytes 1048592 | tf_op jit(solution)/shard_map/psum | solution.py:152
  441.3 34.7 %all-reduce = (bf16[1024]{0:T(1024)(128)(2,1)S(1)}, bf16[1024]{0:T(1024)(128)(2,1)S(1)}) all-reduce(bf16[1024]{0:T(1024)(128)(2,1)S(1)} %get-tuple-element.10, bf16[1024]{0:T(1024)(128)(2,1)S(1)} %copy-done.34), channel_id=1, replica_groups=mesh['ctx'=16,'tp'=2] {'ctx'}, use_global_device_ids=true, to_apply=%region_17.18 | all-reduce | flops 2048 | bytes 8192 | tf_op jit(solution)/shard_map/psum | solution.py:213
  477.2 3.3 fusion.44
  480.5 193.8 %all-reduce.12.cloned.1.call-done = (bf16[1024,3,512]{2,0,1:T(8,128)(2,1)}, bf16[512,1024]{1,0:T(8,128)(2,1)}, bf16[1024,2,1312]{0,2,1:T(8,128)(2,1)}, bf16[1312,1024]{1,0:T(8,128)(2,1)}) async-done(((bf16[1024,3,512]{2,0,1:T(8,128)(2,1)}, bf16[512,1024]{1,0:T(8,128)(2,1)}, bf16[1024,2,1312]{0,2,1:T(8,128)(2,1)}, bf16[1312,1024]{1,0:T(8,128)(2,1)}), (bf16[1024,3,512]{2,0,1:T(8,128)(2,1)}, ...) | async-done | bytes 12255248 | tf_op jit(solution)/shard_map/psum | solution.py:214
  674.3 5.6 convert_element_type.179
  681.6 5.5 convert_element_type.186
  687.1 3.1 convert_element_type.188
  (135 shorter events, 39.4 us)
Async XLA Ops:
  7.2 176.8 %copy-start = (bf16[1312,1024]{1,0:T(8,128)(2,1)S(1)}, bf16[1312,1024]{1,0:T(8,128)(2,1)}, u32[]{:S(2)}) copy-start(bf16[1312,1024]{1,0:T(8,128)(2,1)} %param.16) | copy-start | bytes 8060932
  7.2 4.9 copy-start.1
  7.2 5.4 copy-start.25
  7.2 70.3 %all-gather.4.cloned.1.call-start = ((), (), s32[]{:S(2)}) async-start(), calls=%async_computation.1 | async-start | bytes 4456448 | tf_op jit(solution)/shard_map/all_gather | solution.py:117
  18.0 6.1 copy-start.35
  22.2 108.7 %all-gather.6.cloned.1.call-start = ((), (), s32[]{:S(2)}) async-start(), calls=%async_computation.2 | async-start | bytes 4456448 | tf_op jit(solution)/shard_map/all_gather | solution.py:118
  24.1 152.8 %all-reduce.8.cloned.1.call-start = ((), (), s32[]{:S(2)}) async-start(), calls=%async_computation.3 | async-start | bytes 1048576 | tf_op jit(solution)/shard_map/psum | solution.py:138
  77.5 17.1 %copy-start.4 = (pred[256,4096]{1,0:T(8,128)(4,1)S(1)}, pred[256,4096]{1,0:T(8,128)(4,1)}, u32[]{:S(2)}) copy-start(pred[256,4096]{1,0:T(8,128)(4,1)} %broadcast_compare_fusion) | copy-start | bytes 3145732
  147.2 32.2 %copy-start.24 = (f32[1024]{0:T(1024)S(1)}, f32[1024]{0:T(1024)}, u32[]{:S(2)}) copy-start(f32[1024]{0:T(1024)} %param.14) | copy-start | bytes 12292
  149.8 70.6 %all-reduce.10.cloned.1.call-start = ((), (), s32[]{:S(2)}) async-start(), calls=%async_computation.4 | async-start | bytes 1048576 | tf_op jit(solution)/shard_map/psum | solution.py:165
  179.4 4.5 copy-start.27
  179.4 4.5 copy-start.16
  191.7 203.1 %reduce-scatter.2.cloned.1.call-start = ((), (), s32[]{:S(2)}) async-start(), calls=%async_computation.5 | async-start | bytes 8912896 | tf_op jit(solution)/shard_map/reduce_scatter | solution.py:191
  220.5 5.3 copy-start.8
  291.1 4.9 copy-start.22
  291.1 148.6 %all-reduce.14.cloned.1.call-start = ((), (), s32[]{:S(2)}) async-start(), calls=%async_computation.7 | async-start | bytes 2097152 | tf_op jit(solution)/shard_map/psum | solution.py:152
  399.8 3.9 copy-start.28
  399.8 274.5 %all-reduce.12.cloned.1.call-start = ((), (), s32[]{:S(2)}) async-start(), calls=%async_computation.6 | async-start | bytes 24510464 | tf_op jit(solution)/shard_map/psum | solution.py:214
  399.9 3.8 copy-start.2
  399.9 3.8 copy-start.19
  399.9 3.8 copy-start.21
  403.7 4.2 copy-start.6
  403.7 4.2 copy-start.13
  403.7 5.6 copy-start.10
  403.7 5.6 copy-start.26
  403.7 5.6 copy-start.31
  403.7 5.6 copy-start.33
  412.2 29.1 %copy-start.34 = (bf16[1024]{0:T(1024)(128)(2,1)S(1)}, bf16[1024]{0:T(1024)(128)(2,1)}, u32[]{:S(2)}) copy-start(bf16[1024]{0:T(1024)(128)(2,1)} %get-tuple-element.8) | copy-start | bytes 6148
  674.3 7.2 %slice-start = ((s8[5373952]{0:T(1024)(128)(4,1)}), s8[4194304]{0:T(1024)(128)(4,1)S(1)}, s32[]{:S(2)}) async-start(s8[5373952]{0:T(1024)(128)(4,1)} %bitcast.145), calls=%async_computation.8 | async-start | bytes 8388608
  674.3 5.7 copy-start.17
  674.3 7.2 %slice-start.1 = ((s8[5373952]{0:T(1024)(128)(4,1)}), s8[1179648]{0:T(1024)(128)(4,1)S(1)}, s32[]{:S(2)}) async-start(s8[5373952]{0:T(1024)(128)(4,1)} %bitcast.145), calls=%async_computation.9 | async-start | bytes 2359296
  681.6 5.5 copy-start.12
  (14 other events, 25.5 us)
Sparse Core Ops, SparseCore 0:
  22.3 55.1 all-gather.3
  80.2 50.6 all-gather.5
  149.9 26.8 all-reduce.7
  191.8 28.6 all-reduce.9
  291.2 103.5 reduce-scatter.1
  399.9 39.7 all-reduce.13
  445.0 229.3 all-reduce.11
where the time goes:
time: 706 us; the launch traced here: 697 us
  waiting for transfers between devices  405 us (57%)
  matrix products  135 us (19%)
  other arithmetic  66.6 us (9%)
  blocking collectives  58.1 us (8%)
  local copies, waits for them, and re-layouts  16.6 us (2%)
  between operations  14.8 us (2%)
    psum x1, waiting for transfers between devices, per_device(): lax.psum(grad_w_qkv.astype(jnp.bfloat16), 'ctx').astype(jnp.float32)  194 us
    reduce_scatter x1, waiting for transfers between devices, per_device(): lax.psum_scatter(pair.astype(jnp.bfloat16), 'ctx', scatter_dimension=0, t...  81.5 us
    psum x1, blocking collectives, per_device(): lax.psum(attention_gain_gradient.astype(jnp.bfloat16), 'ctx')  34.7 us
    all_gather x1, waiting for transfers between devices, per_device(): key_piece = lax.all_gather(keys_flat, 'ctx', axis=0, tiled=True)  28.3 us
    psum x1, waiting for transfers between devices, per_device(): lax.psum(ffn_part.astype(jnp.bfloat16), 'tp').astype(jnp.float32)  27.5 us
    psum x1, waiting for transfers between devices, per_device(): lax.psum(second_part.astype(jnp.bfloat16), 'tp').astype(jnp.float32)  27.5 us
    psum x1, waiting for transfers between devices, per_device(): lax.psum(attn_part.astype(jnp.bfloat16), 'tp').astype(jnp.float32)  26.4 us
    all_gather x1, blocking collectives, per_device(): seq_piece = lax.all_gather(seq_ids, 'ctx', axis=0, tiled=True)  23.5 us
  transfers between devices with their start and end apart: 7, of which 7 were waited for; matrix products, arithmetic and copies ran while one was open for 11% of the time, Pallas kernels for 0%

commit v1 on v0

--- a/solution.py
+++ b/solution.py
@@ -3,6 +3,7 @@
 import jax.numpy as jnp
 from jax import lax
 from jax.sharding import PartitionSpec as P
+from jax.lax import all_gather
 
 HD = 64
 EPS = 1e-05
@@ -211,7 +212,7 @@
     grad_tokens = grad_mid + attention_normed_gradient
     summed = (
         lax.psum(attention_gain_gradient.astype(jnp.bfloat16), "ctx").astype(jnp.float32),
-        lax.psum(grad_w_qkv.astype(jnp.bfloat16), "ctx").astype(jnp.float32),
+        jnp.sum(all_gather(grad_w_qkv.astype(jnp.bfloat16), "ctx"), axis=0).astype(jnp.float32),
         lax.psum(grad_w_attn.astype(jnp.bfloat16), "ctx").astype(jnp.float32),
         lax.psum(feedforward_gain_gradient.astype(jnp.bfloat16), "ctx").astype(jnp.float32),
         lax.psum(grad_w_in.astype(jnp.bfloat16), "ctx").astype(jnp.float32),

time: 706 us -> 912 us (1.29)
  waiting for transfers between devices: 405 us -> 587 us
  other arithmetic: 66.6 us -> 89 us
    all_gather x0 -> x1, waiting for transfers between devices: none -> 209 us  [per_device(): all_gather(grad_w_qkv.astype(jnp.bfloat16), 'ctx')]
    psum x1, waiting for transfers between devices: 194 us -> 175 us  [per_device(): lax.psum(grad_w_attn.astype(jnp.bfloat16), 'ctx').astype(jnp.float32)]
    reduce_sum x0 -> x1, other arithmetic: none -> 18.3 us  [per_device(): jnp.sum(all_gather(grad_w_qkv.astype(jnp.bfloat16), 'ctx'), axis=0)]
    reduce_scatter x1, waiting for transfers between devices: 81.5 us -> 71.2 us  [per_device(): lax.psum_scatter(pair.astype(jnp.bfloat16), 'ctx', scatter_dimension=0, t...]
  transfers between devices with their start and end apart: 7 -> 8, of which waited for: 7 -> 8; matrix products, arithmetic and copies ran while one was open for 11% -> 11% of each run, Pallas kernels for 0% -> 0%
where the time goes in v1:
time: 912 us; the launch traced here: 903 us
  waiting for transfers between devices  587 us (64%)
  matrix products  136 us (15%)
  other arithmetic  89 us (10%)
  blocking collectives  57.9 us (6%)
  local copies, waits for them, and re-layouts  16.5 us (2%)
  between operations  15 us (2%)
    all_gather x1, waiting for transfers between devices, per_device(): all_gather(grad_w_qkv.astype(jnp.bfloat16), 'ctx')  209 us
    psum x1, waiting for transfers between devices, per_device(): lax.psum(grad_w_attn.astype(jnp.bfloat16), 'ctx').astype(jnp.float32)  175 us
    reduce_scatter x1, waiting for transfers between devices, per_device(): lax.psum_scatter(pair.astype(jnp.bfloat16), 'ctx', scatter_dimension=0, t...  71.2 us
    psum x1, blocking collectives, per_device(): lax.psum(attention_gain_gradient.astype(jnp.bfloat16), 'ctx')  34.4 us
    psum x1, waiting for transfers between devices, per_device(): lax.psum(ffn_part.astype(jnp.bfloat16), 'tp').astype(jnp.float32)  29 us
    all_gather x1, waiting for transfers between devices, per_device(): key_piece = lax.all_gather(keys_flat, 'ctx', axis=0, tiled=True)  28.3 us
    psum x1, waiting for transfers between devices, per_device(): lax.psum(second_part.astype(jnp.bfloat16), 'tp').astype(jnp.float32)  27.5 us
    psum x1, waiting for transfers between devices, per_device(): lax.psum(attn_part.astype(jnp.bfloat16), 'tp').astype(jnp.float32)  26.4 us
  transfers between devices with their start and end apart: 8, of which 8 were waited for; matrix products, arithmetic and copies ran while one was open for 11% of the time, Pallas kernels for 0%

profile of v1, /device:TPU:0, one launch (start us, length us, event | category | flops | bytes accessed | tf_op | source)
XLA Modules:
  0.0 902.6 jit_solution(1810867299860743567)
XLA Ops:
  7.3 4.8 copy.22
  12.5 3.0 fusion.57
  24.1 23.5 %all-gather.1 = s32[16,1,256]{2,1,0:T(1,128)S(1)} all-gather(s32[1,1,256]{2,1,0:T(1,128)S(1)} %bitcast.163), channel_id=1, replica_groups=mesh['ctx'=16,'tp'=2] {'ctx'}, dimensions={0}, use_global_device_ids=true | all-gather | bytes 17408 | tf_op jit(solution)/shard_map/all_gather | solution.py:120
  49.2 28.3 %all-gather.6.cloned.1.call-done = bf16[4096,512]{0,1:T(8,128)(2,1)} async-done(((bf16[256,512]{0,1:T(8,128)(2,1)}), bf16[4096,512]{0,1:T(8,128)(2,1)}) %all-gather.6.cloned.1.call-update) | async-done | bytes 4194320 | tf_op jit(solution)/shard_map/all_gather | solution.py:118
  77.5 16.5 %select_reduce_fusion = (f32[8,256]{1,0:T(8,128)S(1)}, f32[8,256,4096]{2,1,0:T(8,128)}) fusion(pred[256,4096]{1,0:T(8,128)(4,1)} %broadcast_compare_fusion, bf16[256,8,64]{0,2,1:T(8,128)(2,1)S(1)} %get-tuple-element.37, bf16[4096,8,64]{0,2,1:T(8,128)(2,1)} %bitcast.144), kind=kOutput, calls=%fused_computation.3 | convolution fusion | flops 1098905600 | bytes 39067648 | tf_op jit(solution)/shard_map/qhd,khd->hqk/dot_general | solution.py:124
  94.6 16.2 %fusion = f32[8,256]{1,0:T(8,128)} fusion(f32[8,256,4096]{2,1,0:T(8,128)} %get-tuple-element.43, f32[8,256]{1,0:T(8,128)S(1)} %broadcast_maximum_fusion, pred[256,4096]{1,0:T(8,128)(4,1)S(1)} %copy-done.4), kind=kLoop, calls=%fused_computation.4 | loop fusion | flops 33552384 | bytes 34619392 | tf_op jit(solution)/shard_map/reduce_sum | solution.py:129
  110.8 20.1 %all-gather.8.cloned.1.call-done = bf16[4096,512]{0,1:T(8,128)(2,1)} async-done(((bf16[256,512]{0,1:T(8,128)(2,1)}), bf16[4096,512]{0,1:T(8,128)(2,1)}) %all-gather.8.cloned.1.call-update) | async-done | bytes 4194320 | tf_op jit(solution)/shard_map/all_gather | solution.py:119
  130.9 16.2 %fusion.49 = bf16[256,8,64]{0,2,1:T(8,128)(2,1)} fusion(bf16[4096,8,64]{0,2,1:T(8,128)(2,1)} %bitcast.164, f32[8,256,4096]{2,1,0:T(8,128)} %get-tuple-element.43, f32[8,256]{1,0:T(8,128)} %copy-done.27, pred[256,4096]{1,0:T(8,128)(4,1)} %broadcast_compare_fusion, f32[256,8]{0,1:T(8,128)} %bitcast.161), kind=kOutput, calls=%fused_computation.78 | convolution fusion | flops 1107558400 | bytes 39075840 | tf_op jit(solution)/shard_map/hqk,khd->hqd/dot_general | solution.py:130
  150.2 26.4 %all-reduce.8.cloned.1.call-done = bf16[256,1024]{1,0:T(8,128)(2,1)} async-done(((bf16[256,1024]{1,0:T(8,128)(2,1)}), bf16[256,1024]{1,0:T(8,128)(2,1)}) %all-reduce.8.cloned.1.call-update) | async-done | bytes 524304 | tf_op jit(solution)/shard_map/psum | solution.py:139
  179.3 4.5 fusion.12
  186.4 5.0 fusion.27
  192.8 27.5 %all-reduce.10.cloned.1.call-done = bf16[256,1024]{1,0:T(8,128)(2,1)} async-done(((bf16[256,1024]{1,0:T(8,128)(2,1)}), bf16[256,1024]{1,0:T(8,128)(2,1)}) %all-reduce.10.cloned.1.call-update) | async-done | bytes 524304 | tf_op jit(solution)/shard_map/psum | solution.py:166
  229.6 19.0 %fusion.9 = bf16[8,64,4096]{2,1,0:T(8,128)(2,1)} fusion(bf16[256,8,64]{0,2,1:T(8,128)(2,1)} %bitcast.158, f32[8,256,4096]{2,1,0:T(8,128)} %get-tuple-element.43, f32[8,256]{1,0:T(8,128)} %log_add_fusion, pred[256,4096]{1,0:T(8,128)(4,1)} %broadcast_compare_fusion), kind=kOutput, calls=%fused_computation.13 | convolution fusion | flops 1109393408 | bytes 39067648 | tf_op jit(solution)/shard_map/hqk,qhd->khd/dot_general | solution.py:75
  248.7 23.4 %multiply_convert_fusion = bf16[8,256,4096]{2,1,0:T(8,128)(2,1)} fusion(f32[8,256,4096]{2,1,0:T(8,128)} %get-tuple-element.43, f32[8,256]{1,0:T(8,128)S(1)} %bitcast.162, f32[8,256]{1,0:T(8,128)} %log_add_fusion, pred[256,4096]{1,0:T(8,128)(4,1)} %broadcast_compare_fusion, bf16[256,8,64]{0,2,1:T(8,128)(2,1)} %bitcast.159, bf16[4096,8,64]{0,2,1:T(8,128)(2,1)} %bitcast.165), kind=kOutput, calls=%fused_computation | convolution fusion | flops 1124073472 | bytes 55853056 | tf_op jit(solution)/shard_map/qhd,khd->hqk/dot_general | solution.py:78
  272.1 10.8 %multiply_convert_fusion.1 = bf16[8,64,4096]{2,1,0:T(8,128)(2,1)} fusion(bf16[256,8,64]{0,2,1:T(8,128)(2,1)S(1)} %get-tuple-element.37, bf16[8,256,4096]{2,1,0:T(8,128)(2,1)} %multiply_convert_fusion), kind=kOutput, calls=%fused_computation.12 | convolution fusion | flops 1077936128 | bytes 21233664 | tf_op jit(solution)/shard_map/hqk,qhd->khd/dot_general | solution.py:81
  282.9 7.6 pad_maximum_fusion
  293.7 3.6 convolution_convert_fusion.1
  297.3 4.2 convolution_convert_fusion
  303.0 2.9 convolution_convert_fusion.5
  305.9 14.8 %broadcast_multiply_fusion = (f32[256,8,64]{0,2,1:T(8,128)}, f32[256,8,64]{0,2,1:T(8,128)}) fusion(f32[256,64]{0,1:T(8,128)S(1)} %copy-done.20, bf16[4096,8,64]{0,2,1:T(8,128)(2,1)} %bitcast.145, bf16[8,256,4096]{2,1,0:T(8,128)(2,1)} %multiply_convert_fusion), kind=kOutput, calls=%fused_computation.103 | convolution fusion | flops 1073872896 | bytes 22085632 | tf_op jit(solution)/shard_map/hqk,khd->qhd/dot_general | solution.py:80
  323.1 71.2 %reduce-scatter.2.cloned.1.call-done = bf16[256,2,512]{0,2,1:T(8,128)(2,1)} async-done(((bf16[4096,2,512]{0,2,1:T(8,128)(2,1)}), bf16[256,2,512]{0,2,1:T(8,128)(2,1)}) %reduce-scatter.2.cloned.1.call-update) | async-done | bytes 524304 | tf_op jit(solution)/shard_map/reduce_scatter | solution.py:192
  399.7 4.0 convolution_convert_fusion.2
  403.7 175.3 %all-reduce.12.cloned.1.call-done = (bf16[512,1024]{1,0:T(8,128)(2,1)}, bf16[1024,2,1312]{0,2,1:T(8,128)(2,1)}, bf16[1312,1024]{1,0:T(8,128)(2,1)}) async-done(((bf16[512,1024]{1,0:T(8,128)(2,1)}, bf16[1024,2,1312]{0,2,1:T(8,128)(2,1)}, bf16[1312,1024]{1,0:T(8,128)(2,1)}), (bf16[512,1024]{1,0:T(8,128)(2,1)}, bf16[1024,2,1312]{0,2,1:T(8,128)(2,1)}, ...) | async-done | bytes 9109520 | tf_op jit(solution)/shard_map/psum | solution.py:216
  579.0 2.8 convert_element_type.183
  581.8 8.2 convert_element_type.188
  590.0 3.1 convert_element_type.190
  593.1 29.0 %all-reduce.14.cloned.1.call-done = (bf16[256,1024]{1,0:T(8,128)(2,1)}, bf16[256,1024]{1,0:T(8,128)(2,1)}) async-done(((bf16[256,1024]{1,0:T(8,128)(2,1)}, bf16[256,1024]{1,0:T(8,128)(2,1)}), (bf16[256,1024]{1,0:T(8,128)(2,1)}, bf16[256,1024]{1,0:T(8,128)(2,1)})) %all-reduce.14.cloned.1.call-update) | async-done | bytes 1048592 | tf_op jit(solution)/shard_map/psum | solution.py:153
  623.7 34.4 %all-reduce = (bf16[1024]{0:T(1024)(128)(2,1)S(1)}, bf16[1024]{0:T(1024)(128)(2,1)S(1)}) all-reduce(bf16[1024]{0:T(1024)(128)(2,1)S(1)} %get-tuple-element.10, bf16[1024]{0:T(1024)(128)(2,1)S(1)} %copy-done.32), channel_id=1, replica_groups=mesh['ctx'=16,'tp'=2] {'ctx'}, use_global_device_ids=true, to_apply=%region_17.18 | all-reduce | flops 2048 | bytes 8192 | tf_op jit(solution)/shard_map/psum | solution.py:214
  659.3 3.5 fusion.44
  662.8 208.7 %all-gather.10.cloned.1.call-done = bf16[16384,3,512]{2,0,1:T(8,128)(2,1)} async-done(((bf16[1024,3,512]{2,0,1:T(8,128)(2,1)}), bf16[16384,3,512]{2,0,1:T(8,128)(2,1)}) %all-gather.10.cloned.1.call-update) | async-done | bytes 50331664 | tf_op jit(solution)/shard_map/all_gather | solution.py:215
  871.5 18.3 %reduce_sum.131 = bf16[1024,3,512]{2,0,1:T(8,128)(2,1)} reduce(bf16[16,1024,3,512]{3,1,0,2:T(8,128)(2,1)} %bitcast.143, bf16[]{:T(256)} %constant.46.clone.1), dimensions={0}, to_apply=%region_18.19 | reduce | flops 23592960 | bytes 53477376 | tf_op jit(solution)/shard_map/reduce_sum | solution.py:215
  889.8 5.5 convert_element_type.181
  (130 shorter events, 45.3 us)
Async XLA Ops:
  7.2 176.6 %copy-start = (bf16[1312,1024]{1,0:T(8,128)(2,1)S(1)}, bf16[1312,1024]{1,0:T(8,128)(2,1)}, u32[]{:S(2)}) copy-start(bf16[1312,1024]{1,0:T(8,128)(2,1)} %param.16) | copy-start | bytes 8060932
  7.2 4.9 copy-start.1
  7.2 5.3 copy-start.23
  7.2 70.3 %all-gather.6.cloned.1.call-start = ((), (), s32[]{:S(2)}) async-start(), calls=%async_computation.1 | async-start | bytes 4456448 | tf_op jit(solution)/shard_map/all_gather | solution.py:118
  12.2 3.4 copy-start.28
  12.5 3.1 copy-start.30
  18.0 6.1 copy-start.33
  18.0 3.4 copy-start.14
  22.2 108.7 %all-gather.8.cloned.1.call-start = ((), (), s32[]{:S(2)}) async-start(), calls=%async_computation.2 | async-start | bytes 4456448 | tf_op jit(solution)/shard_map/all_gather | solution.py:119
  24.0 152.6 %all-reduce.8.cloned.1.call-start = ((), (), s32[]{:S(2)}) async-start(), calls=%async_computation.3 | async-start | bytes 1048576 | tf_op jit(solution)/shard_map/psum | solution.py:139
  77.5 17.1 %copy-start.4 = (pred[256,4096]{1,0:T(8,128)(4,1)S(1)}, pred[256,4096]{1,0:T(8,128)(4,1)}, u32[]{:S(2)}) copy-start(pred[256,4096]{1,0:T(8,128)(4,1)} %broadcast_compare_fusion) | copy-start | bytes 3145732
  147.0 32.2 %copy-start.22 = (f32[1024]{0:T(1024)S(1)}, f32[1024]{0:T(1024)}, u32[]{:S(2)}) copy-start(f32[1024]{0:T(1024)} %param.14) | copy-start | bytes 12292
  149.6 70.6 %all-reduce.10.cloned.1.call-start = ((), (), s32[]{:S(2)}) async-start(), calls=%async_computation.4 | async-start | bytes 1048576 | tf_op jit(solution)/shard_map/psum | solution.py:166
  179.2 4.5 copy-start.25
  179.3 4.5 copy-start.15
  191.4 202.9 %reduce-scatter.2.cloned.1.call-start = ((), (), s32[]{:S(2)}) async-start(), calls=%async_computation.5 | async-start | bytes 8912896 | tf_op jit(solution)/shard_map/reduce_scatter | solution.py:192
  220.2 5.3 copy-start.8
  290.6 288.5 %all-reduce.12.cloned.1.call-start = ((), (), s32[]{:S(2)}) async-start(), calls=%async_computation.7 | async-start | bytes 18219008 | tf_op jit(solution)/shard_map/psum | solution.py:216
  293.7 3.6 copy-start.2
  293.7 3.6 copy-start.17
  293.7 3.6 copy-start.19
  293.7 3.6 copy-start.26
  297.3 4.2 copy-start.6
  297.3 4.2 copy-start.12
  302.9 319.2 %all-reduce.14.cloned.1.call-start = ((), (), s32[]{:S(2)}) async-start(), calls=%async_computation.8 | async-start | bytes 2097152 | tf_op jit(solution)/shard_map/psum | solution.py:153
  394.3 3.2 copy-start.10
  396.5 3.2 copy-start.24
  396.5 3.1 copy-start.29
  396.5 3.1 copy-start.31
  399.3 472.2 %all-gather.10.cloned.1.call-start = ((), (), s32[]{:S(2)}) async-start(), calls=%async_computation.6 | async-start | bytes 53477376 | tf_op jit(solution)/shard_map/all_gather | solution.py:215
  581.8 8.2 copy-start.11
  590.0 33.6 %copy-start.32 = (bf16[1024]{0:T(1024)(128)(2,1)S(1)}, bf16[1024]{0:T(1024)(128)(2,1)}, u32[]{:S(2)}) copy-start(bf16[1024]{0:T(1024)(128)(2,1)} %get-tuple-element.8) | copy-start | bytes 6148
  (11 other events, 15.6 us)
Sparse Core Ops, SparseCore 0:
  22.3 55.1 all-gather.5
  80.2 50.6 all-gather.7
  149.8 26.8 all-reduce.7
  191.5 28.6 all-reduce.9
  290.7 103.6 reduce-scatter.1
  398.8 180.1 all-reduce.11
  582.0 40.0 all-reduce.13
  624.2 247.2 all-gather.9
